TPU v7x, 256 devices: a whole 4x4x8 slice. The times are simulated.
256 devices in a mesh: dp: 32 (over y, z), vocab: 8 (over x, core).
Axes of the slice: x: 4, y: 4, z: 8, core: 2. Of those that a mesh axis runs over, the one named last changes fastest.
Arguments:
- draft_logits: bfloat16 [4096, 128000], P('dp', 'vocab'), may hold values from -15 to 250
- hidden: bfloat16 [4096, 2304], P('dp'), may hold values from -40 to 40
- embed_cot: bfloat16 [4096, 2304], P('dp'), may hold values from -0.59765625 to 0.59765625
- draft_ids: int32 [4096], P('dp'), may hold values from 0 to 127999, as said below
- target_ids: int32 [4096, 32], P('dp'), may hold values from 0 to 128255
- target_logits: float32 [4096, 32], P('dp'), may hold values from -8 to 240
- vocab_map: int32 [128256], replicated, may hold values from 0 to 127999
- master: float32 [128000, 2304], P(('vocab', 'dp')), may hold values from -6 to 6
- row_moment: float32 [128000], P(('vocab', 'dp')), may hold values from 0.0001 to 0.5
- col_moment: float32 [2304], replicated, may hold values from 0.003 to 0.03
Outputs:
- direction: bfloat16 [128000, 2304], P(('vocab', 'dp'))
- row_new: float32 [128000], P(('vocab', 'dp'))
- col_new: float32 [2304], replicated
- next_rows: bfloat16 [4096, 2304], P('dp')
Inputs may be any that keep to these rules, and one draw needn't show every extreme that they name: `draft_ids`: among the 128 tokens of one index of dp, at most 20 have draft ids in any one block of 16000 consecutive ids, and some block holds exactly 20 of them.
All inputs are finite; a program needn't handle non-finite values.
Results may differ from a plain program's by a relative error of at most 0.0073.
Values may be sent and summed in bfloat16 or wider, within the bound.
No kernel may reach another device: no remote copies, remote signals or barrier semaphores. Data moves between devices by JAX's collectives and lax.ppermute only.
A program may use at most 128 MiB of HBM per device.

v0:
```python
import jax
import jax.numpy as jnp
from jax import lax
from jax.sharding import PartitionSpec as P

DECAY_RATE = 0.9
STEP_SCALE = 0.01
SQUARE_EPS = 1e-30


def body(
    draft_logits,
    hidden,
    embed_cot,
    draft_ids,
    target_ids,
    target_logits,
    vocab_map,
    master,
    row_moment,
    col_moment,
):
    tokens_here, shard_cols = draft_logits.shape
    owned_rows, features = master.shape
    dp_count = lax.axis_size("dp")
    vocab_count = lax.axis_size("vocab")
    vocab_index = lax.axis_index("vocab")
    dp_index = lax.axis_index("dp")
    logits = draft_logits.astype(jnp.float32)
    local_max = jnp.max(logits, axis=1)
    highest = lax.pmax(local_max, "vocab")
    totals = lax.psum(jnp.sum(jnp.exp(logits - highest[:, None]), axis=1), "vocab")
    probs = jnp.exp(logits - highest[:, None]) / totals[:, None]
    shifted = target_logits - jnp.max(target_logits, axis=1, keepdims=True)
    target_exp = jnp.exp(shifted)
    weights = target_exp / jnp.sum(target_exp, axis=1, keepdims=True)
    mapped = vocab_map[target_ids] - vocab_index * shard_cols
    inside = (mapped >= 0) & (mapped < shard_cols)
    token_index = jnp.broadcast_to(
        jnp.arange(tokens_here, dtype=jnp.int32)[:, None], target_ids.shape
    )
    target = (
        jnp.zeros((tokens_here, shard_cols), jnp.float32)
        .at[token_index, jnp.clip(mapped, 0, shard_cols - 1)]
        .add(jnp.where(inside, weights, jnp.zeros_like(weights)))
    )
    slopes = (probs - target).astype(jnp.bfloat16)
    owned_slopes = lax.all_to_all(slopes, "dp", split_axis=1, concat_axis=0, tiled=True)
    head_grad = jnp.einsum(
        "tv,td->vd",
        owned_slopes,
        lax.all_gather(hidden, "dp", axis=0, tiled=True),
        preferred_element_type=jnp.float32,
    )
    block_base = vocab_index * shard_cols
    in_shard = (draft_ids >= block_base) & (draft_ids < block_base + shard_cols)
    slot_count = tokens_here // vocab_count + tokens_here // (4 * vocab_count)
    position = jnp.cumsum(in_shard.astype(jnp.int32)) - 1
    placing = (position[None, :] == jnp.arange(slot_count, dtype=jnp.int32)[:, None]) & in_shard[
        None, :
    ]
    filled = jnp.any(placing, axis=1)
    packed_ids = jnp.where(filled, jnp.sum(jnp.where(placing, draft_ids[None, :], 0), axis=1), -1)
    placing_half = placing.astype(jnp.bfloat16)
    packed_cot = jnp.dot(placing_half, embed_cot, preferred_element_type=jnp.float32).astype(
        jnp.bfloat16
    )
    all_ids, all_cot = (
        lax.all_gather(packed_ids, "dp", axis=0, tiled=True),
        lax.all_gather(packed_cot, "dp", axis=0, tiled=True),
    )
    row_base = (vocab_index * dp_count + dp_index) * owned_rows
    row_iota = jnp.arange(owned_rows, dtype=jnp.int32)
    matches = (all_ids[None, :] - row_base == row_iota[:, None]).astype(jnp.bfloat16)
    grad = head_grad + jnp.dot(matches, all_cot, preferred_element_type=jnp.float32)
    squares = grad * grad + SQUARE_EPS
    row_new = DECAY_RATE * row_moment + (1.0 - DECAY_RATE) * jnp.mean(squares, axis=1)
    column_total, row_total = lax.psum(
        (jnp.sum(squares, axis=0), jnp.sum(row_new)), ("dp", "vocab")
    )
    vocab_rows = owned_rows * dp_count * vocab_count
    col_new = DECAY_RATE * col_moment + (1.0 - DECAY_RATE) * (column_total / vocab_rows)
    scale = row_new[:, None] * col_new[None, :] / (row_total / vocab_rows)
    direction = grad / jnp.sqrt(scale)
    fresh = (master - STEP_SCALE * direction).astype(jnp.bfloat16)
    wanted = all_ids - row_base
    select = (wanted[:, None] == row_iota[None, :]).astype(jnp.bfloat16)
    slot_values = lax.psum_scatter(
        jnp.dot(select, fresh, preferred_element_type=jnp.float32).astype(jnp.bfloat16),
        "dp",
        scatter_dimension=0,
        tiled=True,
    )
    spread = jnp.einsum("st,sd->td", placing_half, slot_values, preferred_element_type=jnp.float32)
    next_rows = lax.psum(spread.astype(jnp.bfloat16), "vocab")
    return (direction.astype(jnp.bfloat16), row_new, col_new, next_rows)


def solution(mesh):
    in_specs = (
        P("dp", "vocab"),
        P("dp", None),
        P("dp", None),
        P("dp"),
        P("dp", None),
        P("dp", None),
        P(),
        P(("vocab", "dp"), None),
        P(("vocab", "dp")),
        P(),
    )
    out_specs = (P(("vocab", "dp"), None), P(("vocab", "dp")), P(), P("dp", None))
    return jax.shard_map(body, mesh=mesh, in_specs=in_specs, out_specs=out_specs, check_vma=False)
```

profile of v0, /device:TPU:8, one launch (start us, length us, event | category | flops | bytes accessed | tf_op | source)
XLA Modules:
  0.0 619.0 jit_solution(5468428876925927025)
XLA Ops:
  11.0 23.0 %gather_fusion = s32[4096]{0:T(1024)S(1)} fusion(s32[128256]{0:T(1024)S(1)} %copy-done.2, s32[4096]{0:T(1024)S(1)} %broadcast_clamp_fusion), kind=kCustom, calls=%fused_computation | custom fusion | bytes 49152 | tf_op jit(solution)/shard_map/gather | solution.py:37
  35.2 31.6 %scatter_custom_fusion = f32[2048000]{0:T(1024)} fusion(s32[4096]{0:T(1024)S(1)} %reshape.100, f32[4096]{0:T(1024)S(1)} %reshape.102, f32[]{:T(128)} %constant.21.clone.1), kind=kCustom, calls=%fused_computation.10 | custom fusion | flops 4096 | bytes 8192004
  66.8 9.1 %reshape.90 = f32[128,16000]{1,0:T(8,128)} reshape(f32[2048000]{0:T(1024)} %scatter_custom_fusion) | data formatting | bytes 16384000 | tf_op jit(solution)/shard_map/scatter-add | solution.py:45
  78.8 13.1 %pmax.7 = f32[128]{0:T(128)S(1)} all-reduce(bf16[128]{0:T(256)(128)(2,1)S(1)} %reduce_max.23), channel_id=1, replica_groups=mesh['dp'=32,'vocab'=8] {'vocab'}, use_global_device_ids=true, to_apply=%region_1.0 | all-reduce | flops 128 | bytes 768 | tf_op jit(solution)/shard_map/pmax | solution.py:31
  91.9 3.7 fusion.1
  95.5 12.4 %psum.28 = f32[128]{0:T(128)S(1)} all-reduce(f32[128]{0:T(128)S(1)} %fusion.1), channel_id=1, replica_groups=mesh['dp'=32,'vocab'=8] {'vocab'}, use_global_device_ids=true, to_apply=%region_3.0 | all-reduce | flops 128 | bytes 1024 | tf_op jit(solution)/shard_map/psum | solution.py:32
  108.0 6.9 %subtract_convert_fusion = bf16[128,16000]{1,0:T(8,128)(2,1)} fusion(f32[128,16000]{1,0:T(8,128)} %reshape.90, bf16[128,16000]{1,0:T(8,128)(2,1)} %param.10, f32[128]{0:T(128)S(1)} %psum.28, f32[128]{0:T(128)S(1)} %pmax.7), kind=kLoop, calls=%fused_computation.2 | loop fusion | flops 10240000 | bytes 16385024 | tf_op jit(solution)/shard_map/convert_element_type | solution.py:47
  114.9 10.9 %reshape.126 = bf16[128,32,500]{2,1,0:T(8,128)(2,1)} reshape(bf16[128,16000]{1,0:T(8,128)(2,1)} %subtract_convert_fusion) | data formatting | bytes 8192000 | tf_op jit(solution)/shard_map/all_to_all | solution.py:48
  125.7 7.9 %copy.40 = bf16[128,32,500]{0,2,1:T(8,128)(2,1)} copy(bf16[128,32,500]{2,1,0:T(8,128)(2,1)} %reshape.126) | data formatting | bytes 8192000 | tf_op jit(solution)/shard_map/all_to_all | solution.py:48
  133.6 11.5 %all-to-all-start = ((bf16[128,32,500]{0,2,1:T(8,128)(2,1)}), bf16[128,32,500]{0,2,1:T(8,128)(2,1)}, u32[]{:S(2)}, u32[]{:S(2)}) async-start(bf16[128,32,500]{0,2,1:T(8,128)(2,1)} %copy.40), calls=%async_computation | async-start | bytes 8257536 | tf_op jit(solution)/shard_map/all_to_all | solution.py:48
  146.8 146.2 %all-reduce = s32[640]{0:T(1024)S(1)} all-reduce(s32[640]{0:T(1024)S(1)} %select_dynamic-update-slice_fusion), channel_id=1, replica_groups=mesh['dp'=32,'vocab'=8] {'dp'}, use_global_device_ids=true, to_apply=%add | all-reduce | flops 640 | bytes 5120
  293.0 3.8 reshape.123
  296.8 4.1 fusion.8
  301.0 6.6 %copy.38 = bf16[32,128,500]{2,1,0:T(8,128)(2,1)} copy(bf16[32,128,500]{1,2,0:T(8,128)(2,1)} %bitcast) | data formatting | bytes 8192000 | tf_op jit(solution)/shard_map/all_to_all | solution.py:48
  307.5 18.4 %all-gather.4.cloned.1.call-done = bf16[4096,2304]{1,0:T(8,128)(2,1)} async-done(((bf16[128,2304]{1,0:T(8,128)(2,1)}), bf16[4096,2304]{1,0:T(8,128)(2,1)}) %all-gather.4.cloned.1.call-update) | async-done | bytes 18874384 | tf_op jit(solution)/shard_map/all_gather | solution.py:52
  326.0 18.5 %fusion.4 = (f32[2304]{0:T(1024)S(1)}, f32[500]{0:T(512)S(1)}, f32[500,2304]{1,0:T(8,128)}) fusion(f32[500,2304]{1,0:T(8,128)} %fusion.8, bf16[4096,500]{1,0:T(8,128)(2,1)} %bitcast.14, bf16[4096,2304]{1,0:T(8,128)(2,1)} %all-gather.4.cloned.1.call-done), kind=kOutput, calls=%fused_computation.12 | convolution fusion | flops 9442941952 | bytes 32197584 | tf_op jit(solution)/shard_map/tv,td->vd/dot_general | solution.py:49
  345.1 74.8 %all-reduce.3 = (f32[]{:T(128)}, f32[2304]{0:T(1024)S(1)}) all-reduce(f32[]{:T(128)} %get-tuple-element.8, f32[2304]{0:T(1024)S(1)} %get-tuple-element.4), channel_id=1, replica_groups=mesh['dp'=32,'vocab'=8] {'dp','vocab'}, use_global_device_ids=true, to_apply=%region_14.15 | all-reduce | flops 2305 | bytes 18440 | tf_op jit(solution)/shard_map/psum | solution.py:78
  420.6 5.8 convolution_convert_fusion
  426.4 79.6 %fusion = bf16[24,2304]{1,0:T(8,128)(2,1)S(1)} fusion(bf16[640,2304]{1,0:T(8,128)(2,1)S(1)} %convolution_convert_fusion), kind=kCustom, calls=%all-reduce-scatter | all-reduce-scatter fusion | flops 1769473 | bytes 3060736
  510.2 4.7 collective-permute-start.1
  518.1 7.8 %collective-permute-start.3 = (bf16[24,2304]{1,0:T(8,128)(2,1)S(1)}, bf16[24,2304]{1,0:T(8,128)(2,1)S(1)}, u32[]{:S(2)}, u32[]{:S(2)}) collective-permute-start(bf16[24,2304]{1,0:T(8,128)(2,1)S(1)} %fusion), channel_id=1, source_target_pairs={{0,32},{8,40},{16,48},{24,56},{32,64},{40,72},{48,80},{56,88},{64,... | collective-permute-start | bytes 331784
  526.0 8.8 %collective-permute-start.4 = (bf16[24,2304]{1,0:T(8,128)(2,1)S(1)}, bf16[24,2304]{1,0:T(8,128)(2,1)S(1)}, u32[]{:S(2)}, u32[]{:S(2)}) collective-permute-start(bf16[24,2304]{1,0:T(8,128)(2,1)S(1)} %fusion), channel_id=1, source_target_pairs={{0,40},{8,48},{16,56},{24,64},{32,72},{40,80},{48,88},{56,96},{64,... | collective-permute-start | bytes 331784
  541.1 4.5 fusion.23
  545.6 64.9 %all-reduce.6.cloned.1.call-done = bf16[128,2304]{1,0:T(8,128)(2,1)} async-done(((bf16[128,2304]{1,0:T(8,128)(2,1)}), bf16[128,2304]{1,0:T(8,128)(2,1)}) %all-reduce.6.cloned.1.call-update) | async-done | bytes 589840 | tf_op jit(solution)/shard_map/psum | solution.py:95
  (86 shorter events, 24.3 us)
Async XLA Ops:
  7.2 3.8 copy-start.2
  7.2 285.8 %all-gather.6.cloned.1.call-start = ((), (), s32[]{:S(2)}) async-start(), calls=%async_computation.3 | async-start | bytes 3649536 | tf_op jit(solution)/shard_map/all_gather | solution.py:70
  8.0 138.6 %copy-start.9 = (pred[128]{0:T(512)(128)(4,1)}, pred[128]{0:T(512)(128)(4,1)S(1)}, u32[]{:S(2)}) copy-start(pred[128]{0:T(512)(128)(4,1)S(1)} %get-tuple-element.11) | copy-start | bytes 388
  8.4 138.2 %copy-start.8 = (s32[128]{0:T(128)}, s32[128]{0:T(128)S(1)}, u32[]{:S(2)}) copy-start(s32[128]{0:T(128)S(1)} %add_reduce_fusion) | copy-start | bytes 1540
  9.3 316.7 %all-gather.4.cloned.1.call-start = ((), (), s32[]{:S(2)}) async-start(), calls=%async_computation.1 | async-start | bytes 19464192 | tf_op jit(solution)/shard_map/all_gather | solution.py:52
  11.0 23.3 %copy-start.14 = (s32[2]{0:T(128)S(1)}, s32[2]{0:T(128)}, u32[]{:S(2)}) copy-start(s32[2]{0:T(128)} %constant.64) | copy-start | bytes 28
  11.0 23.3 %copy-start.13 = (s32[2]{0:T(128)S(1)}, s32[2]{0:T(128)}, u32[]{:S(2)}) copy-start(s32[2]{0:T(128)} %constant.67) | copy-start | bytes 28
  11.0 23.7 %copy-start.4 = (f32[128,32]{0,1:T(8,128)S(1)}, f32[128,32]{0,1:T(8,128)}, u32[]{:S(2)}) copy-start(f32[128,32]{0,1:T(8,128)} %param.15) | copy-start | bytes 49156
  133.6 11.6 %copy-start.12 = (u32[256]{0:T(256)S(1)}, u32[256]{0:T(256)}, u32[]{:S(2)}) copy-start(u32[256]{0:T(256)} %constant.74) | copy-start | bytes 3076
  133.6 13.0 %copy-start.11 = (s32[128]{0:T(128)S(1)}, s32[128]{0:T(128)}, u32[]{:S(2)}) copy-start(s32[128]{0:T(128)} %param.13) | copy-start | bytes 1540
  133.6 167.3 %all-to-all-start = ((bf16[128,32,500]{0,2,1:T(8,128)(2,1)}), bf16[128,32,500]{0,2,1:T(8,128)(2,1)}, u32[]{:S(2)}, u32[]{:S(2)}) async-start(bf16[128,32,500]{0,2,1:T(8,128)(2,1)} %copy.40), calls=%async_computation | async-start | bytes 8257536 | tf_op jit(solution)/shard_map/all_to_all | solution.py:48
  145.2 465.4 %all-reduce.6.cloned.1.call-start = ((), (), s32[]{:S(2)}) async-start(), calls=%async_computation.2 | async-start | bytes 1179648 | tf_op jit(solution)/shard_map/psum | solution.py:95
  326.0 18.5 %copy-start.10 = (f32[500]{0:T(512)S(1)}, f32[500]{0:T(512)}, u32[]{:S(2)}) copy-start(f32[500]{0:T(512)} %param.18) | copy-start | bytes 6004
  326.0 94.0 %copy-start.6 = (f32[2304]{0:T(1024)S(1)}, f32[2304]{0:T(1024)}, u32[]{:S(2)}) copy-start(f32[2304]{0:T(1024)} %param.19) | copy-start | bytes 27652
  345.1 196.0 %copy-start.7 = (f32[500]{0:T(512)}, f32[500]{0:T(512)S(1)}, u32[]{:S(2)}) copy-start(f32[500]{0:T(512)S(1)} %get-tuple-element.16) | copy-start | bytes 6004
  420.0 121.1 %copy-start.5 = (f32[2304]{0:T(1024)}, f32[2304]{0:T(1024)S(1)}, u32[]{:S(2)}) copy-start(f32[2304]{0:T(1024)S(1)} %multiply_add_fusion.1) | copy-start | bytes 27652
  506.1 29.4 %copy-start.3 = (bf16[24,2304]{1,0:T(8,128)(2,1)}, bf16[24,2304]{1,0:T(8,128)(2,1)S(1)}, u32[]{:S(2)}) copy-start(bf16[24,2304]{1,0:T(8,128)(2,1)S(1)} %fusion) | copy-start | bytes 331780
  506.1 19.9 %collective-permute-start.5 = (bf16[4,2304]{1,0:T(4,128)(2,1)S(1)}, bf16[4,2304]{1,0:T(4,128)(2,1)S(1)}, u32[]{:S(2)}, u32[]{:S(2)}) collective-permute-start(bf16[4,2304]{1,0:T(4,128)(2,1)S(1)} %slice.2), channel_id=1, source_target_pairs={{0,48},{8,56},{16,64},{24,72},{32,80},{40,88},{48,96},{56,104},{64... | collective-permute-start | bytes 55304
  508.0 27.4 %collective-permute-start = (bf16[24,2304]{1,0:T(8,128)(2,1)S(1)}, bf16[24,2304]{1,0:T(8,128)(2,1)S(1)}, u32[]{:S(2)}, u32[]{:S(2)}) collective-permute-start(bf16[24,2304]{1,0:T(8,128)(2,1)S(1)} %fusion), channel_id=1, source_target_pairs={{0,8},{8,16},{16,24},{24,32},{32,40},{40,48},{48,56},{56,64},{64,7... | collective-permute-start | bytes 331784
  510.2 25.3 %collective-permute-start.1 = (bf16[24,2304]{1,0:T(8,128)(2,1)S(1)}, bf16[24,2304]{1,0:T(8,128)(2,1)S(1)}, u32[]{:S(2)}, u32[]{:S(2)}) collective-permute-start(bf16[24,2304]{1,0:T(8,128)(2,1)S(1)} %fusion), channel_id=1, source_target_pairs={{0,16},{8,24},{16,32},{24,40},{32,48},{40,56},{48,64},{56,72},{64,... | collective-permute-start | bytes 331784
  514.9 20.6 %collective-permute-start.2 = (bf16[24,2304]{1,0:T(8,128)(2,1)S(1)}, bf16[24,2304]{1,0:T(8,128)(2,1)S(1)}, u32[]{:S(2)}, u32[]{:S(2)}) collective-permute-start(bf16[24,2304]{1,0:T(8,128)(2,1)S(1)} %fusion), channel_id=1, source_target_pairs={{0,24},{8,32},{16,40},{24,48},{32,56},{40,64},{48,72},{56,80},{64,... | collective-permute-start | bytes 331784
  518.1 17.3 %collective-permute-start.3 = (bf16[24,2304]{1,0:T(8,128)(2,1)S(1)}, bf16[24,2304]{1,0:T(8,128)(2,1)S(1)}, u32[]{:S(2)}, u32[]{:S(2)}) collective-permute-start(bf16[24,2304]{1,0:T(8,128)(2,1)S(1)} %fusion), channel_id=1, source_target_pairs={{0,32},{8,40},{16,48},{24,56},{32,64},{40,72},{48,80},{56,88},{64,... | collective-permute-start | bytes 331784
  526.0 11.1 %collective-permute-start.4 = (bf16[24,2304]{1,0:T(8,128)(2,1)S(1)}, bf16[24,2304]{1,0:T(8,128)(2,1)S(1)}, u32[]{:S(2)}, u32[]{:S(2)}) collective-permute-start(bf16[24,2304]{1,0:T(8,128)(2,1)S(1)} %fusion), channel_id=1, source_target_pairs={{0,40},{8,48},{16,56},{24,64},{32,72},{40,80},{48,88},{56,96},{64,... | collective-permute-start | bytes 331784
  537.1 75.3 %copy-start.1 = (bf16[128,2304]{1,0:T(8,128)(2,1)S(1)}, bf16[128,2304]{1,0:T(8,128)(2,1)}, u32[]{:S(2)}) copy-start(bf16[128,2304]{1,0:T(8,128)(2,1)} %param.12) | copy-start | bytes 1769476
  (1 other events, 1.2 us)
Sparse Core Ops, SparseCore 0:
  11.2 81.9 all-gather.5
  95.7 230.1 all-gather.3
  541.2 69.2 all-reduce.5
where the time goes:
time: 620 us; the launch traced here: 619 us
  blocking collectives  326 us (53%)
  waiting for transfers between devices  85.8 us (14%)
  local copies, waits for them, and re-layouts  66.8 us (11%)
  other arithmetic  52.7 us (8%)
  starting transfers between devices  40.2 us (6%)
  matrix products  31.2 us (5%)
  between operations  16.1 us (3%)
    unnamed x2, blocking collectives  226 us
    psum x1, blocking collectives, body(): lax.psum((jnp.sum(squares, axis=0), jnp.sum(row_new)), ('dp', 'vocab'))  74.8 us
    psum x1, waiting for transfers between devices, body(): next_rows = lax.psum(spread.astype(jnp.bfloat16), 'vocab')  64.9 us
    unnamed x5, other arithmetic  31.9 us
    unnamed x6, starting transfers between devices  28.6 us
    all_to_all x3, local copies, waits for them, and re-layouts, body(): lax.all_to_all(slopes, 'dp', split_axis=1, concat_axis=0, tiled=True)  25.3 us
    gather x1, local copies, waits for them, and re-layouts, body(): mapped = vocab_map[target_ids] - vocab_index * shard_cols  23 us
    dot_general x1, matrix products, body(): jnp.einsum('tv,td->vd', owned_slopes, lax.all_gather(hidden, 'dp', axis=0...  18.5 us
  transfers between devices with their start and end apart: 10, of which 4 were waited for; matrix products, arithmetic and copies ran while one was open for 19% of the time, Pallas kernels for 0%

commit v1 on v0

--- a/solution.py
+++ b/solution.py
@@ -92,7 +92,7 @@
         tiled=True,
     )
     spread = jnp.einsum("st,sd->td", placing_half, slot_values, preferred_element_type=jnp.float32)
-    next_rows = lax.psum(spread.astype(jnp.bfloat16), "vocab")
+    next_rows = jnp.sum(lax.all_gather(spread.astype(jnp.bfloat16), "vocab"), axis=0)
     return (direction.astype(jnp.bfloat16), row_new, col_new, next_rows)
 
 

time: 620 us -> 592 us (0.955)
  waiting for transfers between devices: 85.8 us -> 55.8 us
    psum x1 -> x0, waiting for transfers between devices: 64.9 us -> none  [body(): next_rows = lax.psum(spread.astype(jnp.bfloat16), 'vocab')]
    all_gather x0 -> x1, waiting for transfers between devices: none -> 35.1 us  [body(): lax.all_gather(spread.astype(jnp.bfloat16), 'vocab')]
  transfers between devices with their start and end apart: 10 -> 10, of which waited for: 4 -> 4; matrix products, arithmetic and copies ran while one was open for 19% -> 20% of each run, Pallas kernels for 0% -> 0%
where the time goes in v1:
time: 592 us; the launch traced here: 590 us
  blocking collectives  326 us (55%)
  local copies, waits for them, and re-layouts  64.1 us (11%)
  other arithmetic  56.8 us (10%)
  waiting for transfers between devices  55.8 us (9%)
  starting transfers between devices  40.4 us (7%)
  matrix products  30.5 us (5%)
  between operations  16.1 us (3%)
    unnamed x2, blocking collectives  226 us
    psum x1, blocking collectives, body(): lax.psum((jnp.sum(squares, axis=0), jnp.sum(row_new)), ('dp', 'vocab'))  74.8 us
    all_gather x1, waiting for transfers between devices, body(): lax.all_gather(spread.astype(jnp.bfloat16), 'vocab')  35.1 us
    unnamed x5, other arithmetic  31.9 us
    unnamed x6, starting transfers between devices  28.8 us
    all_to_all x3, local copies, waits for them, and re-layouts, body(): lax.all_to_all(slopes, 'dp', split_axis=1, concat_axis=0, tiled=True)  25.3 us
    gather x1, local copies, waits for them, and re-layouts, body(): mapped = vocab_map[target_ids] - vocab_index * shard_cols  23 us
    dot_general x1, matrix products, body(): jnp.einsum('tv,td->vd', owned_slopes, lax.all_gather(hidden, 'dp', axis=0...  18.5 us
  transfers between devices with their start and end apart: 10, of which 4 were waited for; matrix products, arithmetic and copies ran while one was open for 20% of the time, Pallas kernels for 0%

profile of v1, /device:TPU:8, one launch (start us, length us, event | category | flops | bytes accessed | tf_op | source)
XLA Modules:
  0.0 589.8 jit_solution(11917557533390439845)
XLA Ops:
  11.0 23.0 %gather_fusion = s32[4096]{0:T(1024)S(1)} fusion(s32[128256]{0:T(1024)S(1)} %copy-done.2, s32[4096]{0:T(1024)S(1)} %broadcast_clamp_fusion), kind=kCustom, calls=%fused_computation | custom fusion | bytes 49152 | tf_op jit(solution)/shard_map/gather | solution.py:37
  35.2 31.6 %scatter_custom_fusion = f32[2048000]{0:T(1024)} fusion(s32[4096]{0:T(1024)S(1)} %reshape.100, f32[4096]{0:T(1024)S(1)} %reshape.102, f32[]{:T(128)} %constant.22.clone.1), kind=kCustom, calls=%fused_computation.10 | custom fusion | flops 4096 | bytes 8192004
  66.8 9.1 %reshape.90 = f32[128,16000]{1,0:T(8,128)} reshape(f32[2048000]{0:T(1024)} %scatter_custom_fusion) | data formatting | bytes 16384000 | tf_op jit(solution)/shard_map/scatter-add | solution.py:45
  78.8 13.1 %pmax.7 = f32[128]{0:T(128)S(1)} all-reduce(bf16[128]{0:T(256)(128)(2,1)S(1)} %reduce_max.23), channel_id=1, replica_groups=mesh['dp'=32,'vocab'=8] {'vocab'}, use_global_device_ids=true, to_apply=%region_1.0 | all-reduce | flops 128 | bytes 768 | tf_op jit(solution)/shard_map/pmax | solution.py:31
  95.5 12.4 %psum.21 = f32[128]{0:T(128)S(1)} all-reduce(f32[128]{0:T(128)S(1)} %fusion.1), channel_id=1, replica_groups=mesh['dp'=32,'vocab'=8] {'vocab'}, use_global_device_ids=true, to_apply=%region_3.0 | all-reduce | flops 128 | bytes 1024 | tf_op jit(solution)/shard_map/psum | solution.py:32
  108.0 6.9 %subtract_convert_fusion = bf16[128,16000]{1,0:T(8,128)(2,1)} fusion(f32[128,16000]{1,0:T(8,128)} %reshape.90, bf16[128,16000]{1,0:T(8,128)(2,1)} %param.10, f32[128]{0:T(128)S(1)} %psum.21, f32[128]{0:T(128)S(1)} %pmax.7), kind=kLoop, calls=%fused_computation.2 | loop fusion | flops 10240000 | bytes 16385024 | tf_op jit(solution)/shard_map/convert_element_type | solution.py:47
  114.9 10.9 %reshape.127 = bf16[128,32,500]{2,1,0:T(8,128)(2,1)} reshape(bf16[128,16000]{1,0:T(8,128)(2,1)} %subtract_convert_fusion) | data formatting | bytes 8192000 | tf_op jit(solution)/shard_map/all_to_all | solution.py:48
  125.7 7.9 %copy.40 = bf16[128,32,500]{0,2,1:T(8,128)(2,1)} copy(bf16[128,32,500]{2,1,0:T(8,128)(2,1)} %reshape.127) | data formatting | bytes 8192000 | tf_op jit(solution)/shard_map/all_to_all | solution.py:48
  133.6 11.5 %all-to-all-start = ((bf16[128,32,500]{0,2,1:T(8,128)(2,1)}), bf16[128,32,500]{0,2,1:T(8,128)(2,1)}, u32[]{:S(2)}, u32[]{:S(2)}) async-start(bf16[128,32,500]{0,2,1:T(8,128)(2,1)} %copy.40), calls=%async_computation | async-start | bytes 8257536 | tf_op jit(solution)/shard_map/all_to_all | solution.py:48
  146.8 146.2 %all-reduce = s32[640]{0:T(1024)S(1)} all-reduce(s32[640]{0:T(1024)S(1)} %select_dynamic-update-slice_fusion), channel_id=1, replica_groups=mesh['dp'=32,'vocab'=8] {'dp'}, use_global_device_ids=true, to_apply=%add | all-reduce | flops 640 | bytes 5120
  293.0 3.8 reshape.124
  296.8 4.1 fusion.8
  301.0 6.6 %copy.38 = bf16[32,128,500]{2,1,0:T(8,128)(2,1)} copy(bf16[32,128,500]{1,2,0:T(8,128)(2,1)} %bitcast) | data formatting | bytes 8192000 | tf_op jit(solution)/shard_map/all_to_all | solution.py:48
  307.5 18.4 %all-gather.6.cloned.1.call-done = bf16[4096,2304]{1,0:T(8,128)(2,1)} async-done(((bf16[128,2304]{1,0:T(8,128)(2,1)}), bf16[4096,2304]{1,0:T(8,128)(2,1)}) %all-gather.6.cloned.1.call-update) | async-done | bytes 18874384 | tf_op jit(solution)/shard_map/all_gather | solution.py:52
  326.0 18.5 %fusion.4 = (f32[2304]{0:T(1024)S(1)}, f32[500]{0:T(512)S(1)}, f32[500,2304]{1,0:T(8,128)}) fusion(f32[500,2304]{1,0:T(8,128)} %fusion.8, bf16[4096,500]{1,0:T(8,128)(2,1)} %bitcast.16, bf16[4096,2304]{1,0:T(8,128)(2,1)} %all-gather.6.cloned.1.call-done), kind=kOutput, calls=%fused_computation.12 | convolution fusion | flops 9442941952 | bytes 32197584 | tf_op jit(solution)/shard_map/tv,td->vd/dot_general | solution.py:49
  345.1 74.8 %all-reduce.3 = (f32[]{:T(128)}, f32[2304]{0:T(1024)S(1)}) all-reduce(f32[]{:T(128)} %get-tuple-element.8, f32[2304]{0:T(1024)S(1)} %get-tuple-element.4), channel_id=1, replica_groups=mesh['dp'=32,'vocab'=8] {'dp','vocab'}, use_global_device_ids=true, to_apply=%region_14.15 | all-reduce | flops 2305 | bytes 18440 | tf_op jit(solution)/shard_map/psum | solution.py:78
  420.7 5.8 convolution_convert_fusion
  426.4 79.7 %fusion = bf16[24,2304]{1,0:T(8,128)(2,1)S(1)} fusion(bf16[640,2304]{1,0:T(8,128)(2,1)S(1)} %convolution_convert_fusion), kind=kCustom, calls=%all-reduce-scatter | all-reduce-scatter fusion | flops 1769473 | bytes 3060736
  510.2 4.7 collective-permute-start.1
  518.1 7.8 %collective-permute-start.3 = (bf16[24,2304]{1,0:T(8,128)(2,1)S(1)}, bf16[24,2304]{1,0:T(8,128)(2,1)S(1)}, u32[]{:S(2)}, u32[]{:S(2)}) collective-permute-start(bf16[24,2304]{1,0:T(8,128)(2,1)S(1)} %fusion), channel_id=1, source_target_pairs={{0,32},{8,40},{16,48},{24,56},{32,64},{40,72},{48,80},{56,88},{64,... | collective-permute-start | bytes 331784
  526.0 9.0 %collective-permute-start.4 = (bf16[24,2304]{1,0:T(8,128)(2,1)S(1)}, bf16[24,2304]{1,0:T(8,128)(2,1)S(1)}, u32[]{:S(2)}, u32[]{:S(2)}) collective-permute-start(bf16[24,2304]{1,0:T(8,128)(2,1)S(1)} %fusion), channel_id=1, source_target_pairs={{0,40},{8,48},{16,56},{24,64},{32,72},{40,80},{48,88},{56,96},{64,... | collective-permute-start | bytes 331784
  539.7 4.5 fusion.23
  544.2 35.1 %all-gather.8.cloned.1.call-done = bf16[1024,2304]{1,0:T(8,128)(2,1)} async-done(((bf16[128,2304]{1,0:T(8,128)(2,1)}), bf16[1024,2304]{1,0:T(8,128)(2,1)}) %all-gather.8.cloned.1.call-update) | async-done | bytes 4718608 | tf_op jit(solution)/shard_map/all_gather | solution.py:95
  579.3 4.0 reduce_sum.72
  (88 shorter events, 24.3 us)
Async XLA Ops:
  7.2 285.8 %all-gather.10.cloned.1.call-start = ((), (), s32[]{:S(2)}) async-start(), calls=%async_computation.3 | async-start | bytes 3649536 | tf_op jit(solution)/shard_map/all_gather | solution.py:70
  8.0 138.6 %copy-start.9 = (pred[128]{0:T(512)(128)(4,1)}, pred[128]{0:T(512)(128)(4,1)S(1)}, u32[]{:S(2)}) copy-start(pred[128]{0:T(512)(128)(4,1)S(1)} %get-tuple-element.11) | copy-start | bytes 388
  8.4 138.2 %copy-start.7 = (s32[128]{0:T(128)}, s32[128]{0:T(128)S(1)}, u32[]{:S(2)}) copy-start(s32[128]{0:T(128)S(1)} %add_reduce_fusion) | copy-start | bytes 1540
  9.3 316.7 %all-gather.6.cloned.1.call-start = ((), (), s32[]{:S(2)}) async-start(), calls=%async_computation.1 | async-start | bytes 19464192 | tf_op jit(solution)/shard_map/all_gather | solution.py:52
  11.0 23.3 %copy-start.15 = (s32[2]{0:T(128)S(1)}, s32[2]{0:T(128)}, u32[]{:S(2)}) copy-start(s32[2]{0:T(128)} %constant.66) | copy-start | bytes 28
  11.0 23.3 %copy-start.14 = (s32[2]{0:T(128)S(1)}, s32[2]{0:T(128)}, u32[]{:S(2)}) copy-start(s32[2]{0:T(128)} %constant.69) | copy-start | bytes 28
  11.0 23.7 %copy-start.3 = (f32[128,32]{0,1:T(8,128)S(1)}, f32[128,32]{0,1:T(8,128)}, u32[]{:S(2)}) copy-start(f32[128,32]{0,1:T(8,128)} %param.15) | copy-start | bytes 49156
  133.6 11.6 %copy-start.13 = (u32[256]{0:T(256)S(1)}, u32[256]{0:T(256)}, u32[]{:S(2)}) copy-start(u32[256]{0:T(256)} %constant.76) | copy-start | bytes 3076
  133.6 13.0 %copy-start.12 = (s32[128]{0:T(128)S(1)}, s32[128]{0:T(128)}, u32[]{:S(2)}) copy-start(s32[128]{0:T(128)} %param.13) | copy-start | bytes 1540
  133.6 167.3 %all-to-all-start = ((bf16[128,32,500]{0,2,1:T(8,128)(2,1)}), bf16[128,32,500]{0,2,1:T(8,128)(2,1)}, u32[]{:S(2)}, u32[]{:S(2)}) async-start(bf16[128,32,500]{0,2,1:T(8,128)(2,1)} %copy.40), calls=%async_computation | async-start | bytes 8257536 | tf_op jit(solution)/shard_map/all_to_all | solution.py:48
  145.2 434.2 %all-gather.8.cloned.1.call-start = ((), (), s32[]{:S(2)}) async-start(), calls=%async_computation.2 | async-start | bytes 5308416 | tf_op jit(solution)/shard_map/all_gather | solution.py:95
  326.0 18.5 %copy-start.11 = (f32[500]{0:T(512)S(1)}, f32[500]{0:T(512)}, u32[]{:S(2)}) copy-start(f32[500]{0:T(512)} %param.18) | copy-start | bytes 6004
  326.0 94.0 %copy-start.5 = (f32[2304]{0:T(1024)S(1)}, f32[2304]{0:T(1024)}, u32[]{:S(2)}) copy-start(f32[2304]{0:T(1024)} %param.19) | copy-start | bytes 27652
  345.1 194.5 %copy-start.6 = (f32[500]{0:T(512)}, f32[500]{0:T(512)S(1)}, u32[]{:S(2)}) copy-start(f32[500]{0:T(512)S(1)} %get-tuple-element.9) | copy-start | bytes 6004
  420.0 119.7 %copy-start.4 = (f32[2304]{0:T(1024)}, f32[2304]{0:T(1024)S(1)}, u32[]{:S(2)}) copy-start(f32[2304]{0:T(1024)S(1)} %multiply_add_fusion.1) | copy-start | bytes 27652
  420.6 117.8 %copy-start.8 = (s32[128]{0:T(128)S(1)}, s32[128]{0:T(128)}, u32[]{:S(2)}) copy-start(s32[128]{0:T(128)} %copy-done.7) | copy-start | bytes 1540
  420.6 117.8 %copy-start.10 = (pred[128]{0:T(512)(128)(4,1)S(1)}, pred[128]{0:T(512)(128)(4,1)}, u32[]{:S(2)}) copy-start(pred[128]{0:T(512)(128)(4,1)} %copy-done.9) | copy-start | bytes 388
  506.1 19.9 %collective-permute-start.5 = (bf16[4,2304]{1,0:T(4,128)(2,1)S(1)}, bf16[4,2304]{1,0:T(4,128)(2,1)S(1)}, u32[]{:S(2)}, u32[]{:S(2)}) collective-permute-start(bf16[4,2304]{1,0:T(4,128)(2,1)S(1)} %slice.2), channel_id=1, source_target_pairs={{0,48},{8,56},{16,64},{24,72},{32,80},{40,88},{48,96},{56,104},{64... | collective-permute-start | bytes 55304
  508.0 27.6 %collective-permute-start = (bf16[24,2304]{1,0:T(8,128)(2,1)S(1)}, bf16[24,2304]{1,0:T(8,128)(2,1)S(1)}, u32[]{:S(2)}, u32[]{:S(2)}) collective-permute-start(bf16[24,2304]{1,0:T(8,128)(2,1)S(1)} %fusion), channel_id=1, source_target_pairs={{0,8},{8,16},{16,24},{24,32},{32,40},{40,48},{48,56},{56,64},{64,7... | collective-permute-start | bytes 331784
  510.2 25.5 %collective-permute-start.1 = (bf16[24,2304]{1,0:T(8,128)(2,1)S(1)}, bf16[24,2304]{1,0:T(8,128)(2,1)S(1)}, u32[]{:S(2)}, u32[]{:S(2)}) collective-permute-start(bf16[24,2304]{1,0:T(8,128)(2,1)S(1)} %fusion), channel_id=1, source_target_pairs={{0,16},{8,24},{16,32},{24,40},{32,48},{40,56},{48,64},{56,72},{64,... | collective-permute-start | bytes 331784
  514.9 20.9 %collective-permute-start.2 = (bf16[24,2304]{1,0:T(8,128)(2,1)S(1)}, bf16[24,2304]{1,0:T(8,128)(2,1)S(1)}, u32[]{:S(2)}, u32[]{:S(2)}) collective-permute-start(bf16[24,2304]{1,0:T(8,128)(2,1)S(1)} %fusion), channel_id=1, source_target_pairs={{0,24},{8,32},{16,40},{24,48},{32,56},{40,64},{48,72},{56,80},{64,... | collective-permute-start | bytes 331784
  518.1 17.6 %collective-permute-start.3 = (bf16[24,2304]{1,0:T(8,128)(2,1)S(1)}, bf16[24,2304]{1,0:T(8,128)(2,1)S(1)}, u32[]{:S(2)}, u32[]{:S(2)}) collective-permute-start(bf16[24,2304]{1,0:T(8,128)(2,1)S(1)} %fusion), channel_id=1, source_target_pairs={{0,32},{8,40},{16,48},{24,56},{32,64},{40,72},{48,80},{56,88},{64,... | collective-permute-start | bytes 331784
  526.0 11.1 %collective-permute-start.4 = (bf16[24,2304]{1,0:T(8,128)(2,1)S(1)}, bf16[24,2304]{1,0:T(8,128)(2,1)S(1)}, u32[]{:S(2)}, u32[]{:S(2)}) collective-permute-start(bf16[24,2304]{1,0:T(8,128)(2,1)S(1)} %fusion), channel_id=1, source_target_pairs={{0,40},{8,48},{16,56},{24,64},{32,72},{40,80},{48,88},{56,96},{64,... | collective-permute-start | bytes 331784
  539.6 43.6 %copy-start.1 = (bf16[128,2304]{1,0:T(8,128)(2,1)S(1)}, bf16[128,2304]{1,0:T(8,128)(2,1)}, u32[]{:S(2)}) copy-start(bf16[128,2304]{1,0:T(8,128)(2,1)} %param.12) | copy-start | bytes 1769476
  (2 other events, 5.0 us)
Sparse Core Ops, SparseCore 0:
  11.2 81.9 all-gather.9
  95.7 230.1 all-gather.5
  539.7 39.5 all-gather.7
